TPU v7x, 32 devices: a whole 2x2x4 slice. The times are simulated.
32 devices in a mesh: ctx: 4 (over z), fsdp: 8 (over y, x, core).
Axes of the slice: x: 2, y: 2, z: 4, core: 2. Of those that a mesh axis runs over, the one named last changes fastest.
Arguments:
- tokens: bfloat16 [8, 1024, 2048], P('fsdp', 'ctx'), may hold values from -6 to 6
- attn_gain: bfloat16 [2048], P('fsdp'), may hold values from 0.25 to 1.75
- w_query: bfloat16 [2048, 2048], P('fsdp'), may hold values from -1.2374369 to 1.2374369
- w_key: bfloat16 [2048, 256], P('fsdp'), may hold values from -0.13258252 to 0.13258252
- w_value: bfloat16 [2048, 256], P('fsdp'), may hold values from -0.125 to 0.125
- w_out: bfloat16 [2048, 2048], P('fsdp'), may hold values from -1.5 to 1.5
- ffn_gain: bfloat16 [2048], P('fsdp'), may hold values from 0.25 to 1.75
- w_gate: bfloat16 [2048, 5632], P('fsdp'), may hold values from -0.125 to 0.125
- w_up: bfloat16 [2048, 5632], P('fsdp'), may hold values from -0.125 to 0.125
- w_down: bfloat16 [5632, 2048], P('fsdp'), may hold values from -0.078125 to 0.078125
- block_table: int32 [4, 2], replicated, may hold values from 0 to 7, as said below
- positions: int32 [8, 1024], P('fsdp', 'ctx'), may hold values from 0 to 5118, as said below
- out_grad: bfloat16 [8, 1024, 2048], P('fsdp', 'ctx'), may hold values from -6 to 6
Outputs:
- layer_out: bfloat16 [8, 1024, 2048], P('fsdp', 'ctx')
- tokens_grad: float32 [8, 1024, 2048], P('fsdp', 'ctx')
- attn_gain_grad: float32 [2048], P('fsdp')
- w_query_grad: float32 [2048, 2048], P('fsdp')
- w_key_grad: float32 [2048, 256], P('fsdp')
- w_value_grad: float32 [2048, 256], P('fsdp')
- w_out_grad: float32 [2048, 2048], P('fsdp')
- ffn_gain_grad: float32 [2048], P('fsdp')
- w_gate_grad: float32 [2048, 5632], P('fsdp')
- w_up_grad: float32 [2048, 5632], P('fsdp')
- w_down_grad: float32 [5632, 2048], P('fsdp')
Inputs may be any that keep to these rules, and one draw needn't show every extreme that they name: `block_table`: row c holds a block p and its mirror 8 - 1 - p; every block of 0 to 7 stands once in the table. positions[s, r] is an offset of sequence s plus idx of stored row r, so positions rise by one along a sequence.
All inputs are finite; a program needn't handle non-finite values.
Results may differ from a plain program's by a relative error of at most 0.014.
Values may be sent and summed in bfloat16 or wider, within the bound.
A program may use at most 512 MiB of HBM per device.

v0:
```python
import jax
import jax.numpy as jnp
from jax import lax
from jax.sharding import PartitionSpec as P

HEADS = 32
KV_HEADS = 4
HEAD_DIM = 64
EPS = 1e-05
THETA = 10000.0


def rope_tables(positions):
    half_dim = HEAD_DIM // 2
    frequency = THETA ** (-jnp.arange(half_dim, dtype=jnp.float32) * (2.0 / HEAD_DIM))
    angle = positions.astype(jnp.float32)[:, None] * frequency[None, :]
    return (jnp.cos(angle)[:, None, :], jnp.sin(angle)[:, None, :])


def rotate(values, cosine, sine):
    half_dim = HEAD_DIM // 2
    first = values[..., :half_dim]
    second = values[..., half_dim:]
    return jnp.concatenate(
        [first * cosine - second * sine, second * cosine + first * sine], axis=-1
    )


def unrotate(grads, cosine, sine):
    half_dim = HEAD_DIM // 2
    first = grads[..., :half_dim]
    second = grads[..., half_dim:]
    return jnp.concatenate(
        [first * cosine + second * sine, second * cosine - first * sine], axis=-1
    )


def contract_rows(left, right):
    return lax.dot_general(
        left, right, (((0,), (0,)), ((), ())), preferred_element_type=jnp.float32
    )


def times_transpose(left, right):
    return lax.dot_general(
        left, right, (((1,), (1,)), ((), ())), preferred_element_type=jnp.float32
    )


def shards(
    tokens,
    attn_gain,
    w_query,
    w_key,
    w_value,
    w_out,
    ffn_gain,
    w_gate,
    w_up,
    w_down,
    block_table,
    positions,
    out_grad,
):
    inputs = tokens[0].astype(jnp.float32)
    cotangent = out_grad[0].astype(jnp.float32)
    local_rows = inputs.shape[0]
    model_width = inputs.shape[1]
    hidden_width = w_gate.shape[1]
    group_size = HEADS // KV_HEADS
    query_width = HEADS * HEAD_DIM
    key_width = KV_HEADS * HEAD_DIM
    score_scale = HEAD_DIM ** (-0.5)
    cosine, sine = rope_tables(positions[0])
    block_rows = local_rows // 2
    seq_index = (
        block_table[:, :, None] * block_rows
        + jnp.arange(block_rows, dtype=jnp.int32)[None, None, :]
    ).reshape(-1)
    own_index = lax.dynamic_slice_in_dim(seq_index, lax.axis_index("ctx") * local_rows, local_rows)
    allowed = seq_index[None, :] <= own_index[:, None]
    inverse_one = lax.rsqrt(jnp.mean(inputs * inputs, axis=1, keepdims=True) + EPS)
    unit_one = inputs * inverse_one
    gain_piece = lax.all_gather(attn_gain, "fsdp", axis=0, tiled=True)
    query_piece = lax.all_gather(w_query, "fsdp", axis=0, tiled=True)
    key_piece = lax.all_gather(w_key, "fsdp", axis=0, tiled=True)
    value_piece = lax.all_gather(w_value, "fsdp", axis=0, tiled=True)
    out_piece = lax.all_gather(w_out, "fsdp", axis=0, tiled=True)
    columns = (unit_one * gain_piece.astype(jnp.float32)[None, :]).astype(jnp.bfloat16)
    query_sum = jnp.dot(columns, query_piece, preferred_element_type=jnp.float32)
    key_sum = jnp.dot(columns, key_piece, preferred_element_type=jnp.float32)
    value_sum = jnp.dot(columns, value_piece, preferred_element_type=jnp.float32)
    normed = columns
    out_full = out_piece
    query_sum, key_sum, value_sum, normed_one, out_full = (
        query_sum,
        key_sum,
        value_sum,
        normed,
        out_full,
    )
    queries_low = rotate(query_sum.reshape(local_rows, HEADS, HEAD_DIM), cosine, sine).astype(
        jnp.bfloat16
    )
    keys_low = (
        rotate(key_sum.reshape(local_rows, KV_HEADS, HEAD_DIM), cosine, sine)
        .reshape(local_rows, key_width)
        .astype(jnp.bfloat16)
    )
    values_low = value_sum.astype(jnp.bfloat16)
    keys_all, values_all = (
        lax.all_gather(keys_low, "ctx", axis=0, tiled=True),
        lax.all_gather(values_low, "ctx", axis=0, tiled=True),
    )
    seq_length = keys_all.shape[0]
    query_heads = queries_low.reshape(local_rows, KV_HEADS, group_size, HEAD_DIM).transpose(
        1, 2, 0, 3
    )
    key_heads = keys_all.reshape(seq_length, KV_HEADS, HEAD_DIM).transpose(1, 0, 2)
    value_heads = values_all.reshape(seq_length, KV_HEADS, HEAD_DIM).transpose(1, 0, 2)

    def scores_of(query_one, key_block):
        raw = times_transpose(query_one, key_block) * score_scale
        return jnp.where(allowed, raw, -1e30)

    def head_forward(operands):
        query_block, key_block, value_block = operands

        def single(query_one):
            scores = scores_of(query_one, key_block)
            highest = jnp.max(scores, axis=-1, keepdims=True)
            weights = jnp.exp(scores - highest)
            totals = jnp.sum(weights, axis=-1, keepdims=True)
            softmaxed = (weights / totals).astype(jnp.bfloat16)
            mixed = jnp.dot(softmaxed, value_block, preferred_element_type=jnp.float32)
            return (mixed, highest[:, 0] + jnp.log(totals[:, 0]))

        return lax.map(single, query_block)

    mixed_heads, log_totals = lax.map(head_forward, (query_heads, key_heads, value_heads))
    attended = (
        mixed_heads.transpose(2, 0, 1, 3).reshape(local_rows, query_width).astype(jnp.bfloat16)
    )
    hidden_one = inputs + jnp.dot(attended, out_full, preferred_element_type=jnp.float32)
    inverse_two = lax.rsqrt(jnp.mean(hidden_one * hidden_one, axis=1, keepdims=True) + EPS)
    unit_two = hidden_one * inverse_two
    gain_piece = lax.all_gather(ffn_gain, "fsdp", axis=0, tiled=True)
    gate_piece = lax.all_gather(w_gate, "fsdp", axis=0, tiled=True)
    up_piece = lax.all_gather(w_up, "fsdp", axis=0, tiled=True)
    columns = (unit_two * gain_piece.astype(jnp.float32)[None, :]).astype(jnp.bfloat16)
    gate_sum = jnp.dot(columns, gate_piece, preferred_element_type=jnp.float32)
    up_sum = jnp.dot(columns, up_piece, preferred_element_type=jnp.float32)
    sigmoid_gate = jax.nn.sigmoid(gate_sum)
    silu_gate = gate_sum * sigmoid_gate
    activated = (silu_gate * up_sum).astype(jnp.bfloat16)
    branch_out = jnp.dot(
        activated,
        lax.all_gather(w_down, "fsdp", axis=0, tiled=True),
        preferred_element_type=jnp.float32,
    )
    layer_out = (hidden_one + branch_out).astype(jnp.bfloat16)
    grad_branch = cotangent.astype(jnp.bfloat16)
    grad_activated = times_transpose(
        grad_branch, lax.all_gather(w_down, "fsdp", axis=0, tiled=True)
    )
    grad_gate = (
        grad_activated * up_sum * sigmoid_gate * (1.0 + gate_sum * (1.0 - sigmoid_gate))
    ).astype(jnp.bfloat16)
    grad_up = (grad_activated * silu_gate).astype(jnp.bfloat16)
    gain_piece = lax.all_gather(ffn_gain, "fsdp", axis=0, tiled=True)
    gate_piece = lax.all_gather(w_gate, "fsdp", axis=0, tiled=True)
    up_piece = lax.all_gather(w_up, "fsdp", axis=0, tiled=True)
    grad_cols = times_transpose(grad_gate, gate_piece) + times_transpose(grad_up, up_piece)
    gain_grad = jnp.sum(grad_cols * unit_two, axis=0)
    grad_unit = grad_cols * gain_piece.astype(jnp.float32)[None, :]
    grad_unit_two = grad_unit
    gain_grad_two = gain_grad
    grad_gate_up = jnp.concatenate([grad_gate, grad_up], axis=1)
    down_shard = lax.psum_scatter(
        contract_rows(activated, grad_branch), "fsdp", scatter_dimension=0, tiled=True
    )
    gate_up_shard = lax.psum_scatter(
        contract_rows(columns, grad_gate_up), "fsdp", scatter_dimension=0, tiled=True
    )
    grad_hidden = cotangent + inverse_two * (
        grad_unit_two - unit_two * jnp.mean(grad_unit_two * unit_two, axis=1, keepdims=True)
    )
    grad_attn_low = grad_hidden.astype(jnp.bfloat16)
    grad_attended = times_transpose(
        grad_attn_low, lax.all_gather(w_out, "fsdp", axis=0, tiled=True)
    ).astype(jnp.bfloat16)
    out_term = contract_rows(attended, grad_attn_low)
    grad_heads = grad_attended.reshape(local_rows, KV_HEADS, group_size, HEAD_DIM).transpose(
        1, 2, 0, 3
    )

    def head_backward(operands):
        query_block, key_block, value_block, grad_block, log_block = operands

        def single(carry, items):
            key_total, value_total = carry
            query_one, grad_one, log_one = items
            scores = scores_of(query_one, key_block)
            softmaxed = jnp.exp(scores - log_one[:, None])
            grad_probs = times_transpose(grad_one, value_block)
            inner = jnp.sum(softmaxed * grad_probs, axis=-1, keepdims=True)
            grad_scores = (softmaxed * (grad_probs - inner)).astype(jnp.bfloat16)
            grad_query = (
                jnp.dot(grad_scores, key_block, preferred_element_type=jnp.float32) * score_scale
            )
            key_total = key_total + contract_rows(grad_scores, query_one) * score_scale
            value_total = value_total + contract_rows(softmaxed.astype(jnp.bfloat16), grad_one)
            return ((key_total, value_total), grad_query)

        start_totals = (
            jnp.zeros((seq_length, HEAD_DIM), jnp.float32),
            jnp.zeros((seq_length, HEAD_DIM), jnp.float32),
        )
        (key_total, value_total), grad_query = lax.scan(
            single, start_totals, (query_block, grad_block, log_block)
        )
        return (grad_query, key_total, value_total)

    grad_query_heads, grad_key_heads, grad_value_heads = lax.map(
        head_backward, (query_heads, key_heads, value_heads, grad_heads, log_totals)
    )
    grad_keys_all = grad_key_heads.transpose(1, 0, 2).reshape(seq_length, key_width)
    grad_values_all = grad_value_heads.transpose(1, 0, 2).reshape(seq_length, key_width)
    own_key_grad, own_value_grad = (
        lax.psum_scatter(grad_keys_all, "ctx", scatter_dimension=0, tiled=True),
        lax.psum_scatter(grad_values_all, "ctx", scatter_dimension=0, tiled=True),
    )
    grad_key_low = (
        unrotate(own_key_grad.reshape(local_rows, KV_HEADS, HEAD_DIM), cosine, sine)
        .reshape(local_rows, key_width)
        .astype(jnp.bfloat16)
    )
    grad_value_low = own_value_grad.astype(jnp.bfloat16)
    grad_query_rows = grad_query_heads.transpose(2, 0, 1, 3).reshape(local_rows, HEADS, HEAD_DIM)
    grad_query_low = (
        unrotate(grad_query_rows, cosine, sine)
        .reshape(local_rows, query_width)
        .astype(jnp.bfloat16)
    )
    gain_piece = lax.all_gather(attn_gain, "fsdp", axis=0, tiled=True)
    query_piece = lax.all_gather(w_query, "fsdp", axis=0, tiled=True)
    key_piece = lax.all_gather(w_key, "fsdp", axis=0, tiled=True)
    value_piece = lax.all_gather(w_value, "fsdp", axis=0, tiled=True)
    grad_cols = (
        times_transpose(grad_query_low, query_piece)
        + times_transpose(grad_key_low, key_piece)
        + times_transpose(grad_value_low, value_piece)
    )
    gain_grad = jnp.sum(grad_cols * unit_one, axis=0)
    grad_unit = grad_cols * gain_piece.astype(jnp.float32)[None, :]
    tokens_grad = grad_hidden + inverse_one * (
        grad_unit - unit_one * jnp.mean(grad_unit * unit_one, axis=1, keepdims=True)
    )
    query_term = contract_rows(normed_one, grad_query_low)
    key_term = contract_rows(normed_one, grad_key_low)
    value_term = contract_rows(normed_one, grad_value_low)
    gain_one_shard, gain_two_shard, query_shard, key_shard, value_shard, out_shard = (
        lax.psum_scatter(gain_grad, "fsdp", scatter_dimension=0, tiled=True),
        lax.psum_scatter(gain_grad_two, "fsdp", scatter_dimension=0, tiled=True),
        lax.psum_scatter(query_term, "fsdp", scatter_dimension=0, tiled=True),
        lax.psum_scatter(key_term, "fsdp", scatter_dimension=0, tiled=True),
        lax.psum_scatter(value_term, "fsdp", scatter_dimension=0, tiled=True),
        lax.psum_scatter(out_term, "fsdp", scatter_dimension=0, tiled=True),
    )
    gate_shard = gate_up_shard[:, :hidden_width]
    up_shard = gate_up_shard[:, hidden_width:]
    summed = lax.psum(
        (
            gain_one_shard,
            query_shard,
            key_shard,
            value_shard,
            out_shard,
            gain_two_shard,
            gate_shard,
            up_shard,
            down_shard,
        ),
        "ctx",
    )
    return (
        layer_out.reshape(1, local_rows, model_width),
        tokens_grad.reshape(1, local_rows, model_width),
        summed[0],
        summed[1],
        summed[2],
        summed[3],
        summed[4],
        summed[5],
        summed[6],
        summed[7],
        summed[8],
    )


def solution(mesh):
    return jax.shard_map(
        shards,
        mesh=mesh,
        in_specs=(
            P("fsdp", "ctx", None),
            P("fsdp"),
            P("fsdp", None),
            P("fsdp", None),
            P("fsdp", None),
            P("fsdp", None),
            P("fsdp"),
            P("fsdp", None),
            P("fsdp", None),
            P("fsdp", None),
            P(),
            P("fsdp", "ctx"),
            P("fsdp", "ctx", None),
        ),
        out_specs=(
            P("fsdp", "ctx", None),
            P("fsdp", "ctx", None),
            P("fsdp"),
            P("fsdp", None),
            P("fsdp", None),
            P("fsdp", None),
            P("fsdp", None),
            P("fsdp"),
            P("fsdp", None),
            P("fsdp", None),
            P("fsdp", None),
        ),
        check_vma=False,
    )
```

profile of v0, /device:TPU:0, one launch (start us, length us, event | category | flops | bytes accessed | tf_op | source)
XLA Modules:
  0.0 3205.1 jit_solution(12606878503554546676)
XLA Ops:
  13.1 10.4 all-gather
  24.0 8.9 all-gather.1
  33.2 3.0 all-gather.12.cloned.1.call-done
  38.3 16.1 all_gather.45
  54.8 6.7 all-gather.14.cloned.1.call-done
  63.3 16.6 all_gather.47
  81.4 36.5 %all-gather.10.cloned.1.call-done = bf16[2048,2048]{1,0:T(8,128)(2,1)} async-done(((bf16[256,2048]{1,0:T(8,128)(2,1)}), bf16[2048,2048]{1,0:T(8,128)(2,1)}) %all-gather.10.cloned.1.call-update) | async-done | bytes 8388624 | tf_op jit(solution)/shard_map/all_gather | solution.py:85
  117.9 12.3 copy.43
  130.3 5.8 fusion.60
  139.9 4.7 maximum_bitcast_fusion
  144.6 60.9 %while.64 = (s32[]{:T(128)}, bf16[4,8,256,64]{2,3,1,0:T(8,128)(2,1)}, f32[4,8,256]{2,1,0:T(8,128)S(1)}, bf16[4,8,256,64]{3,2,1,0:T(8,128)(2,1)}, bf16[4,1024,64]...) while((s32[]{:T(128)}, ...), condition=%wide.region_6.7_spmd.clone.clone, body=%wide.region_1.6_spmd.clone.sunk.clone | while | flops 69467904 | bytes 6454618 | solution.py:140
  147.6 11.5 while.63
  162.8 11.5 while.63
  178.1 11.6 while.63
  193.4 11.4 while.63
  206.5 6.2 multiply_reduce_fusion.3
  212.9 79.4 %all-gather.18.cloned.1.call-done = bf16[2048,5632]{1,0:T(8,128)(2,1)} async-done(((bf16[256,5632]{1,0:T(8,128)(2,1)}), bf16[2048,5632]{1,0:T(8,128)(2,1)}) %all-gather.18.cloned.1.call-update) | async-done | bytes 23068688 | tf_op jit(solution)/shard_map/all_gather | solution.py:148
  292.4 13.5 fusion.81
  305.8 104.8 %all-gather.20.cloned.1.call-done = bf16[2048,5632]{1,0:T(8,128)(2,1)} async-done(((bf16[256,5632]{1,0:T(8,128)(2,1)}), bf16[2048,5632]{1,0:T(8,128)(2,1)}) %all-gather.20.cloned.1.call-update) | async-done | bytes 23068688 | tf_op jit(solution)/shard_map/all_gather | solution.py:149
  410.6 13.6 fusion.82
  424.2 104.7 %all-gather.22.cloned.1.call-done = bf16[5632,2048]{1,0:T(8,128)(2,1)} async-done(((bf16[704,2048]{1,0:T(8,128)(2,1)}), bf16[5632,2048]{1,0:T(8,128)(2,1)}) %all-gather.22.cloned.1.call-update) | async-done | bytes 23068688 | tf_op jit(solution)/shard_map/all_gather | solution.py:158
  529.0 18.5 multiply_convert_fusion.1
  547.5 12.5 fusion.83
  560.0 14.0 multiply_reduce_fusion.1
  574.0 2.2 multiply_add_fusion
  577.5 5.8 convolution_convert_fusion
  583.8 168.1 %while.66 = (s32[]{:T(128)}, f32[4,8,256,64]{2,3,1,0:T(8,128)}, f32[4,1024,64]{1,2,0:T(8,128)}, f32[4,1024,64]{1,2,0:T(8,128)}, bf16[4,8,256,64]{3,2,1,0:T(8,128...) while((s32[]{:T(128)}, f32[4,8,256,64]{2,3,1,0:T(8,128)}, ...), condition=%wide.region_13.14_spmd.clone.clone, body=%wide.region_9.13_spmd.clone.sunk.clone | while | flops 170737408 | bytes 22899168 | solution.py:224
  583.9 2.2 dynamic-slice_bitcast_fusion.21
  588.6 34.4 %while.65 = (s32[]{:T(128)}, f32[1024,64]{0,1:T(8,128)S(1)}, f32[1024,64]{0,1:T(8,128)S(1)}, f32[8,256,64]{1,2,0:T(8,128)}, bf16[8,256,64]{2,1,0:T(8,128)(2,1)},...) while((s32[]{:T(128)}, f32[1024,64]{0,1:T(8,128)S(1)}, ...), condition=%wide.region_12.12_spmd.clone, body=%wide.region_10.11_spmd.clone.sunk | while | flops 170475264 | bytes 10032288 | solution.py:219
  623.0 1.9 bitcast_dynamic-update-slice_fusion.15
  625.8 2.3 dynamic-slice_bitcast_fusion.21
  630.6 34.4 %while.65 = (s32[]{:T(128)}, f32[1024,64]{0,1:T(8,128)S(1)}, f32[1024,64]{0,1:T(8,128)S(1)}, f32[8,256,64]{1,2,0:T(8,128)}, bf16[8,256,64]{2,1,0:T(8,128)(2,1)},...) while((s32[]{:T(128)}, f32[1024,64]{0,1:T(8,128)S(1)}, ...), condition=%wide.region_12.12_spmd.clone, body=%wide.region_10.11_spmd.clone.sunk | while | flops 170475264 | bytes 10032288 | solution.py:219
  665.0 2.0 bitcast_dynamic-update-slice_fusion.15
  667.9 2.3 dynamic-slice_bitcast_fusion.21
  672.6 34.4 %while.65 = (s32[]{:T(128)}, f32[1024,64]{0,1:T(8,128)S(1)}, f32[1024,64]{0,1:T(8,128)S(1)}, f32[8,256,64]{1,2,0:T(8,128)}, bf16[8,256,64]{2,1,0:T(8,128)(2,1)},...) while((s32[]{:T(128)}, f32[1024,64]{0,1:T(8,128)S(1)}, ...), condition=%wide.region_12.12_spmd.clone, body=%wide.region_10.11_spmd.clone.sunk | while | flops 170475264 | bytes 10032288 | solution.py:219
  707.0 2.0 bitcast_dynamic-update-slice_fusion.15
  709.9 2.3 dynamic-slice_bitcast_fusion.21
  714.6 34.4 %while.65 = (s32[]{:T(128)}, f32[1024,64]{0,1:T(8,128)S(1)}, f32[1024,64]{0,1:T(8,128)S(1)}, f32[8,256,64]{1,2,0:T(8,128)}, bf16[8,256,64]{2,1,0:T(8,128)(2,1)},...) while((s32[]{:T(128)}, f32[1024,64]{0,1:T(8,128)S(1)}, ...), condition=%wide.region_12.12_spmd.clone, body=%wide.region_10.11_spmd.clone.sunk | while | flops 170475264 | bytes 10032288 | solution.py:219
  749.0 1.9 bitcast_dynamic-update-slice_fusion.15
  753.1 34.9 %fusion.30 = f32[2048,11264]{1,0:T(8,128)} fusion(bf16[256,2048]{1,0:T(8,128)(2,1)S(1)} %copy-done.14, bf16[256,5632]{1,0:T(8,128)(2,1)} %get-tuple-element.429, bf16[256,5632]{1,0:T(8,128)(2,1)} %get-tuple-element.430), kind=kOutput, calls=%fused_computation.55 | convolution fusion | flops 11822694400 | bytes 99090432 | tf_op jit(solution)/shard_map/dot_general | solution.py:39
  791.9 15.6 reduce-scatter.10.cloned.1.call-done
  807.4 2.9 fusion.69
  812.2 9.0 fusion.64
  822.9 9.6 fusion.66
  832.5 21.7 fusion.54
  856.1 983.4 %all-reduce.9.cloned.1.call-done = f32[2048,11264]{1,0:T(8,128)} async-done(((f32[2048,11264]{1,0:T(8,128)}), f32[2048,11264]{1,0:T(8,128)}) %all-reduce.9.cloned.1.call-update) | async-done | bytes 92274704
  1839.6 10.4 fusion.80
  1850.0 35.5 %reduce-scatter.14.cloned.1.call-done = f32[256,256]{1,0:T(8,128)} async-done(((f32[2048,256]{1,0:T(8,128)}), f32[256,256]{1,0:T(8,128)}) %reduce-scatter.14.cloned.1.call-update) | async-done | bytes 262160 | tf_op jit(solution)/shard_map/reduce_scatter | solution.py:266
  1885.5 45.0 %reduce-scatter.16.cloned.1.call-done = f32[256,256]{1,0:T(8,128)} async-done(((f32[2048,256]{1,0:T(8,128)}), f32[256,256]{1,0:T(8,128)}) %reduce-scatter.16.cloned.1.call-update) | async-done | bytes 262160 | tf_op jit(solution)/shard_map/reduce_scatter | solution.py:267
  1930.4 119.9 %reduce-scatter.12.cloned.1.call-done = f32[256,2048]{1,0:T(8,128)} async-done(((f32[2048,2048]{1,0:T(8,128)}), f32[256,2048]{1,0:T(8,128)}) %reduce-scatter.12.cloned.1.call-update) | async-done | bytes 2097168 | tf_op jit(solution)/shard_map/reduce_scatter | solution.py:265
  2050.4 119.8 %reduce-scatter.18.cloned.1.call-done = f32[256,2048]{1,0:T(8,128)} async-done(((f32[2048,2048]{1,0:T(8,128)}), f32[256,2048]{1,0:T(8,128)}) %reduce-scatter.18.cloned.1.call-update) | async-done | bytes 2097168 | tf_op jit(solution)/shard_map/reduce_scatter | solution.py:268
  2170.2 268.2 %reduce-scatter.20.cloned.1.call-done = f32[704,2048]{1,0:T(8,128)} async-done(((f32[5632,2048]{1,0:T(8,128)}), f32[704,2048]{1,0:T(8,128)}) %reduce-scatter.20.cloned.1.call-update) | async-done | bytes 5767184 | tf_op jit(solution)/shard_map/reduce_scatter | solution.py:179
  2438.5 6.2 fusion.84
  2444.7 13.5 fusion.43
  2459.6 2.3 fusion.50
  2461.9 24.6 all-reduce.3
  2486.6 13.0 all-reduce.4
  2499.6 3.5 fusion.49
  2503.1 676.1 %all-reduce.11.cloned.1.call-done = (f32[256,2048]{1,0:T(8,128)}, f32[256,256]{1,0:T(8,128)}, f32[256,256]{1,0:T(8,128)}, f32[256,2048]{1,0:T(8,128)}, f32[256,5...) async-done(((f32[256,2048]{1,0:T(8,128)}, f32[256,256]{1,0:T(8,128)}, f32[256,256]{1,0:T(8,128)}, f32[256,2048]{1,0:T(8,128)}, f32[256,5632]{1,0:T(8,128)}, ...) | async-done | bytes 22020112 | tf_op jit(solution)/shard_map/psum | solution.py:272
  3179.2 3.3 copy.125
  3182.5 2.0 copy.126
  3187.5 2.9 copy.129
  3192.3 2.8 copy.130
  3195.8 2.5 copy.131
  (682 shorter events, 245.0 us)
Async XLA Ops:
  7.2 29.0 all-gather.12.cloned.1.call-start
  7.9 53.7 %all-gather.14.cloned.1.call-start = ((), (), s32[]{:S(2)}) async-start(), calls=%async_computation.9 | async-start | bytes 1179648 | tf_op jit(solution)/shard_map/all_gather | solution.py:87
  8.7 109.2 %all-gather.10.cloned.1.call-start = ((), (), s32[]{:S(2)}) async-start(), calls=%async_computation.7 | async-start | bytes 9437184 | tf_op jit(solution)/shard_map/all_gather | solution.py:85
  9.4 196.1 %all-gather.16.cloned.1.call-start = ((), (), s32[]{:S(2)}) async-start(), calls=%async_computation.10 | async-start | bytes 9437184 | tf_op jit(solution)/shard_map/all_gather | solution.py:88
  10.0 282.4 %all-gather.18.cloned.1.call-start = ((), (), s32[]{:S(2)}) async-start(), calls=%async_computation.11 | async-start | bytes 25952256 | tf_op jit(solution)/shard_map/all_gather | solution.py:148
  10.6 400.0 %all-gather.20.cloned.1.call-start = ((), (), s32[]{:S(2)}) async-start(), calls=%async_computation.12 | async-start | bytes 25952256 | tf_op jit(solution)/shard_map/all_gather | solution.py:149
  11.1 2.0 copy-start.33
  11.1 12.3 copy-start
  11.2 12.7 copy-start.31
  11.2 12.7 copy-start.32
  11.2 12.9 copy-start.34
  11.2 517.8 %all-gather.22.cloned.1.call-start = ((), (), s32[]{:S(2)}) async-start(), calls=%async_computation.13 | async-start | bytes 25952256 | tf_op jit(solution)/shard_map/all_gather | solution.py:158
  11.9 776.2 %reduce-scatter.8.cloned.1.call-start = ((), (), s32[]{:S(2)}) async-start(), calls=%async_computation.14 | async-start | bytes 1310720 | tf_op jit(solution)/shard_map/reduce_scatter | solution.py:230
  23.5 106.8 %copy-start.26 = (f32[8,1,256]{2,1,0:T(1,128)}, f32[8,1,256]{2,1,0:T(1,128)S(1)}, u32[]{:S(2)}) copy-start(f32[8,1,256]{2,1,0:T(1,128)S(1)} %convert_element_type.151) | copy-start | bytes 24580
  23.8 106.4 %copy-start.28 = (f32[256]{0:T(256)}, f32[256]{0:T(256)S(1)}, u32[]{:S(2)}) copy-start(f32[256]{0:T(256)S(1)} %add_rsqrt_fusion.1) | copy-start | bytes 3076
  33.1 103.0 %copy-start.22 = (f32[256,32]{0,1:T(8,128)}, f32[256,32]{0,1:T(8,128)S(1)}, u32[]{:S(2)}) copy-start(f32[256,32]{0,1:T(8,128)S(1)} %get-tuple-element.440) | copy-start | bytes 98308
  33.1 103.0 %copy-start.24 = (f32[256,32]{0,1:T(8,128)}, f32[256,32]{0,1:T(8,128)S(1)}, u32[]{:S(2)}) copy-start(f32[256,32]{0,1:T(8,128)S(1)} %get-tuple-element.441) | copy-start | bytes 98308
  147.6 1.0 copy-start.7
  164.3 1.0 copy-start.7
  167.1 1.0 copy-start.7
  170.1 1.0 copy-start.7
  182.3 1.0 copy-start.7
  183.8 1.0 copy-start.7
  185.3 1.0 copy-start.7
  186.8 1.0 copy-start.7
  188.2 1.0 copy-start.7
  205.5 1.0 copy-start.6
  212.7 361.3 %copy-start.4 = (f32[256,2048]{1,0:T(8,128)}, f32[256,2048]{1,0:T(8,128)S(1)}, u32[]{:S(2)}) copy-start(f32[256,2048]{1,0:T(8,128)S(1)} %get-tuple-element.443) | copy-start | bytes 6291460
  212.9 197.7 %copy-start.13 = (bf16[256,2048]{1,0:T(8,128)(2,1)}, bf16[256,2048]{1,0:T(8,128)(2,1)S(1)}, u32[]{:S(2)}) copy-start(bf16[256,2048]{1,0:T(8,128)(2,1)S(1)} %multiply_convert_fusion.4) | copy-start | bytes 3145732
  560.0 14.0 copy-start.17
  576.2 1.3 copy-start.2
  583.8 4.8 copy-start.10
  623.0 2.8 copy-start.11
  625.8 4.8 copy-start.10
  665.0 2.8 copy-start.11
  667.9 4.8 copy-start.10
  707.0 2.8 copy-start.11
  709.9 4.8 copy-start.10
  749.0 2.8 copy-start.11
  751.9 1.2 copy-start.14
  751.9 55.5 %reduce-scatter.10.cloned.1.call-start = ((), (), s32[]{:S(2)}) async-start(), calls=%async_computation.15 | async-start | bytes 1310720 | tf_op jit(solution)/shard_map/reduce_scatter | solution.py:231
  752.6 1087.0 %all-reduce.9.cloned.1.call-start = ((), (), s32[]{:S(2)}) async-start(), calls=%async_computation.21 | async-start | bytes 184549376
  788.0 1.8 copy-start.1
  788.0 1.8 copy-start.27
  788.0 1.8 copy-start.29
  788.1 1097.4 %reduce-scatter.14.cloned.1.call-start = ((), (), s32[]{:S(2)}) async-start(), calls=%async_computation.17 | async-start | bytes 2359296 | tf_op jit(solution)/shard_map/reduce_scatter | solution.py:266
  791.8 19.0 copy-start.18
  791.8 1138.6 %reduce-scatter.16.cloned.1.call-start = ((), (), s32[]{:S(2)}) async-start(), calls=%async_computation.18 | async-start | bytes 2359296 | tf_op jit(solution)/shard_map/reduce_scatter | solution.py:267
  810.3 1240.1 %reduce-scatter.12.cloned.1.call-start = ((), (), s32[]{:S(2)}) async-start(), calls=%async_computation.16 | async-start | bytes 18874368 | tf_op jit(solution)/shard_map/reduce_scatter | solution.py:265
  811.2 1.0 copy-start.15
  821.2 1.7 copy-start.3
  821.2 1349.0 %reduce-scatter.18.cloned.1.call-start = ((), (), s32[]{:S(2)}) async-start(), calls=%async_computation.19 | async-start | bytes 18874368 | tf_op jit(solution)/shard_map/reduce_scatter | solution.py:268
  832.5 1605.9 %reduce-scatter.20.cloned.1.call-start = ((), (), s32[]{:S(2)}) async-start(), calls=%async_computation.20 | async-start | bytes 51904512 | tf_op jit(solution)/shard_map/reduce_scatter | solution.py:179
  854.3 2324.9 %all-reduce.11.cloned.1.call-start = ((), (), s32[]{:S(2)}) async-start(), calls=%async_computation.22 | async-start | bytes 44040192 | tf_op jit(solution)/shard_map/psum | solution.py:272
  2438.4 6.3 copy-start.5
  2438.5 6.3 copy-start.12
  2444.7 13.5 copy-start.16
  2458.3 1.3 copy-start.21
  2459.6 2.3 copy-start.30
  3179.2 7.0 copy-start.19
  3179.2 8.3 copy-start.9
  3187.5 4.7 copy-start.8
  3187.5 7.5 slice-start
  3192.3 3.6 slice-start.1
  (27 other events, 25.1 us)
Sparse Core Ops, SparseCore 0:
  9.9 26.2 all-gather.11
  38.1 23.4 all-gather.13
  63.5 54.3 all-gather.9
  119.6 54.3 all-gather.15
  175.8 116.4 all-gather.17
  294.1 116.4 all-gather.19
  412.5 116.4 all-gather.21
  752.0 27.1 reduce-scatter.7
  781.6 25.7 reduce-scatter.9
  811.1 1028.4 all-reduce.8
  1843.8 41.6 reduce-scatter.13
  1889.2 41.1 reduce-scatter.15
  1934.4 115.9 reduce-scatter.11
  2054.2 115.9 reduce-scatter.17
  2174.1 264.2 reduce-scatter.19
  2442.3 736.8 all-reduce.10
where the time goes:
time: 3210 us
  waiting for transfers between devices  2600 us (81%)
  matrix products  349 us (11%)
  local copies, waits for them, and re-layouts  110 us (3%)
  blocking collectives  89.4 us (3%)
  other arithmetic  33.1 us (1%)
    unnamed x17, waiting for transfers between devices  989 us
    psum x1, waiting for transfers between devices, shards(): lax.psum((gain_one_shard, query_shard, key_shard, value_shard, out_shard,...  676 us
    reduce_scatter x1, waiting for transfers between devices, shards(): lax.psum_scatter(contract_rows(activated, grad_branch), 'fsdp', scatter_d...  268 us
    dot_general x103, matrix products, times_transpose(): lax.dot_general(left, right, (((1,), (1,)), ((), ())), preferred_element_...  128 us
    dot_general x70, matrix products, contract_rows(): lax.dot_general(left, right, (((0,), (0,)), ((), ())), preferred_element_...  124 us
    reduce_scatter x1, waiting for transfers between devices, shards(): lax.psum_scatter(query_term, 'fsdp', scatter_dimension=0, tiled=True)  120 us
    reduce_scatter x1, waiting for transfers between devices, shards(): lax.psum_scatter(out_term, 'fsdp', scatter_dimension=0, tiled=True)  120 us
    all_gather x1, waiting for transfers between devices, shards(): up_piece = lax.all_gather(w_up, 'fsdp', axis=0, tiled=True)  105 us
  transfers between devices with their start and end apart: 16, of which 14 were waited for; matrix products, arithmetic and copies ran while one was open for 7% of the time, Pallas kernels for 0%

commit v1 on v0

--- a/solution.py
+++ b/solution.py
@@ -8,6 +8,27 @@
 HEAD_DIM = 64
 EPS = 1e-05
 THETA = 10000.0
+
+
+def laid_out(blocks, dim):
+    shape = list(blocks.shape[1:])
+    shape[dim] *= blocks.shape[0]
+    return jnp.moveaxis(blocks, 0, dim).reshape(shape)
+
+
+def collected_by_bits(shard, axis):
+    size, here = (lax.axis_size(axis), lax.axis_index(axis))
+    blocks, bit = (shard[None], 1)
+    while bit < size:
+        other = lax.ppermute(blocks, axis, [(i, i ^ bit) for i in range(size)])
+        low = here & bit == 0
+        blocks = jnp.concatenate([jnp.where(low, blocks, other), jnp.where(low, other, blocks)])
+        bit *= 2
+    return blocks
+
+
+def doubled_up(array, axis, dim):
+    return laid_out(collected_by_bits(array, axis), dim)
 
 
 def rope_tables(positions):
@@ -154,9 +175,7 @@
     silu_gate = gate_sum * sigmoid_gate
     activated = (silu_gate * up_sum).astype(jnp.bfloat16)
     branch_out = jnp.dot(
-        activated,
-        lax.all_gather(w_down, "fsdp", axis=0, tiled=True),
-        preferred_element_type=jnp.float32,
+        activated, doubled_up(w_down, "fsdp", 0), preferred_element_type=jnp.float32
     )
     layer_out = (hidden_one + branch_out).astype(jnp.bfloat16)
     grad_branch = cotangent.astype(jnp.bfloat16)

time: 3210 us -> 3340 us (1.040)
  other arithmetic: 33.1 us -> 86.1 us
  waiting for transfers between devices: 2600 us -> 2650 us
    psum x1, waiting for transfers between devices: 676 us -> 379 us  [shards(): lax.psum((gain_one_shard, query_shard, key_shard, value_shard, out_shard,...]
    ppermute x0 -> x3, waiting for transfers between devices: none -> 254 us  [collected_by_bits(): other = lax.ppermute(blocks, axis, [(i, i ^ bit) for i in range(size)])]
    unnamed x17, waiting for transfers between devices: 989 us -> 1100 us
  transfers between devices with their start and end apart: 16 -> 19, of which waited for: 14 -> 16; matrix products, arithmetic and copies ran while one was open for 7% -> 10% of each run, Pallas kernels for 0% -> 0%
where the time goes in v1:
time: 3340 us; the launch traced here: 3330 us
  waiting for transfers between devices  2650 us (79%)
  matrix products  380 us (11%)
  local copies, waits for them, and re-layouts  103 us (3%)
  blocking collectives  88.8 us (3%)
  other arithmetic  86.1 us (3%)
    unnamed x17, waiting for transfers between devices  1100 us
    psum x1, waiting for transfers between devices, shards(): lax.psum((gain_one_shard, query_shard, key_shard, value_shard, out_shard,...  379 us
    reduce_scatter x1, waiting for transfers between devices, shards(): lax.psum_scatter(contract_rows(activated, grad_branch), 'fsdp', scatter_d...  268 us
    ppermute x3, waiting for transfers between devices, collected_by_bits(): other = lax.ppermute(blocks, axis, [(i, i ^ bit) for i in range(size)])  254 us
    dot_general x103, matrix products, times_transpose(): lax.dot_general(left, right, (((1,), (1,)), ((), ())), preferred_element_...  127 us
    dot_general x70, matrix products, contract_rows(): lax.dot_general(left, right, (((0,), (0,)), ((), ())), preferred_element_...  124 us
    reduce_scatter x1, waiting for transfers between devices, shards(): lax.psum_scatter(query_term, 'fsdp', scatter_dimension=0, tiled=True)  120 us
    reduce_scatter x1, waiting for transfers between devices, shards(): lax.psum_scatter(out_term, 'fsdp', scatter_dimension=0, tiled=True)  120 us
  transfers between devices with their start and end apart: 19, of which 16 were waited for; matrix products, arithmetic and copies ran while one was open for 10% of the time, Pallas kernels for 0%

profile of v1, /device:TPU:0, one launch (start us, length us, event | category | flops | bytes accessed | tf_op | source)
XLA Modules:
  0.0 3328.3 jit_solution(6152382535046860093)
XLA Ops:
  12.2 10.3 all-gather
  23.1 8.9 all-gather.1
  32.3 3.9 all-gather.12.cloned.1.call-done
  38.2 16.1 all_gather.44
  55.6 5.9 all-gather.14.cloned.1.call-done
  63.3 16.6 all_gather.46
  81.4 36.5 %all-gather.10.cloned.1.call-done = bf16[2048,2048]{1,0:T(8,128)(2,1)} async-done(((bf16[256,2048]{1,0:T(8,128)(2,1)}), bf16[2048,2048]{1,0:T(8,128)(2,1)}) %all-gather.10.cloned.1.call-update) | async-done | bytes 8388624 | tf_op jit(solution)/shard_map/all_gather | solution.py:106
  117.8 12.4 copy.43
  130.3 5.9 fusion.60
  140.0 4.7 maximum_bitcast_fusion
  144.7 81.6 %while.64 = (s32[]{:T(128)}, bf16[4,8,256,64]{2,3,1,0:T(8,128)(2,1)S(1)}, f32[4,8,256]{2,1,0:T(8,128)S(1)}, bf16[4,8,256,64]{3,2,1,0:T(8,128)(2,1)}, bf16[4,1024...) while((s32[]{:T(128)}, ...), condition=%wide.region_6.7_spmd.clone.clone, body=%wide.region_1.6_spmd.clone.sunk.clone | while | flops 69467904 | bytes 5799230 | solution.py:161
  147.8 17.2 while.63
  168.2 17.2 while.63
  188.7 17.1 while.63
  209.0 17.2 while.63
  227.4 7.5 multiply_reduce_fusion.3
  235.2 57.0 %all-gather.18.cloned.1.call-done = bf16[2048,5632]{1,0:T(8,128)(2,1)} async-done(((bf16[256,5632]{1,0:T(8,128)(2,1)}), bf16[2048,5632]{1,0:T(8,128)(2,1)}) %all-gather.18.cloned.1.call-update) | async-done | bytes 23068688 | tf_op jit(solution)/shard_map/all_gather | solution.py:169
  292.3 13.5 fusion.81
  305.7 104.8 %all-gather.20.cloned.1.call-done = bf16[2048,5632]{1,0:T(8,128)(2,1)} async-done(((bf16[256,5632]{1,0:T(8,128)(2,1)}), bf16[2048,5632]{1,0:T(8,128)(2,1)}) %all-gather.20.cloned.1.call-update) | async-done | bytes 23068688 | tf_op jit(solution)/shard_map/all_gather | solution.py:170
  410.5 13.6 fusion.82
  424.1 104.7 %all-gather.22.cloned.1.call-done = bf16[5632,2048]{1,0:T(8,128)(2,1)} async-done(((bf16[704,2048]{1,0:T(8,128)(2,1)}), bf16[5632,2048]{1,0:T(8,128)(2,1)}) %all-gather.22.cloned.1.call-update) | async-done | bytes 23068688 | tf_op jit(solution)/shard_map/all_gather | solution.py:183
  528.9 18.5 multiply_convert_fusion.1
  547.4 12.5 fusion.83
  559.9 14.0 multiply_reduce_fusion.1
  573.9 2.2 multiply_add_fusion
  577.4 5.7 convolution_convert_fusion
  584.5 169.9 %while.66 = (s32[]{:T(128)}, f32[4,8,256,64]{2,3,1,0:T(8,128)}, f32[4,1024,64]{1,2,0:T(8,128)}, f32[4,1024,64]{1,2,0:T(8,128)}, bf16[4,8,256,64]{3,2,1,0:T(8,128...) while((s32[]{:T(128)}, f32[4,8,256,64]{2,3,1,0:T(8,128)}, ...), condition=%wide.region_13.14_spmd.clone.clone, body=%wide.region_9.13_spmd.clone.sunk.clone | while | flops 170737408 | bytes 14510505 | solution.py:243
  589.8 34.4 %while.65 = (s32[]{:T(128)}, f32[1024,64]{0,1:T(8,128)S(1)}, f32[1024,64]{0,1:T(8,128)S(1)}, f32[8,256,64]{1,2,0:T(8,128)}, bf16[8,256,64]{2,1,0:T(8,128)(2,1)},...) while((s32[]{:T(128)}, f32[1024,64]{0,1:T(8,128)S(1)}, ...), condition=%wide.region_12.12_spmd.clone, body=%wide.region_10.11_spmd.clone.sunk | while | flops 170475264 | bytes 10032288 | solution.py:238
  632.3 34.4 %while.65 = (s32[]{:T(128)}, f32[1024,64]{0,1:T(8,128)S(1)}, f32[1024,64]{0,1:T(8,128)S(1)}, f32[8,256,64]{1,2,0:T(8,128)}, bf16[8,256,64]{2,1,0:T(8,128)(2,1)},...) while((s32[]{:T(128)}, f32[1024,64]{0,1:T(8,128)S(1)}, ...), condition=%wide.region_12.12_spmd.clone, body=%wide.region_10.11_spmd.clone.sunk | while | flops 170475264 | bytes 10032288 | solution.py:238
  674.8 34.4 %while.65 = (s32[]{:T(128)}, f32[1024,64]{0,1:T(8,128)S(1)}, f32[1024,64]{0,1:T(8,128)S(1)}, f32[8,256,64]{1,2,0:T(8,128)}, bf16[8,256,64]{2,1,0:T(8,128)(2,1)},...) while((s32[]{:T(128)}, f32[1024,64]{0,1:T(8,128)S(1)}, ...), condition=%wide.region_12.12_spmd.clone, body=%wide.region_10.11_spmd.clone.sunk | while | flops 170475264 | bytes 10032288 | solution.py:238
  717.3 34.4 %while.65 = (s32[]{:T(128)}, f32[1024,64]{0,1:T(8,128)S(1)}, f32[1024,64]{0,1:T(8,128)S(1)}, f32[8,256,64]{1,2,0:T(8,128)}, bf16[8,256,64]{2,1,0:T(8,128)(2,1)},...) while((s32[]{:T(128)}, f32[1024,64]{0,1:T(8,128)S(1)}, ...), condition=%wide.region_12.12_spmd.clone, body=%wide.region_10.11_spmd.clone.sunk | while | flops 170475264 | bytes 10032288 | solution.py:238
  755.2 35.1 %fusion.30 = f32[2048,11264]{1,0:T(8,128)} fusion(bf16[256,2048]{1,0:T(8,128)(2,1)} %copy-done.14, bf16[256,5632]{1,0:T(8,128)(2,1)} %get-tuple-element.431, bf16[256,5632]{1,0:T(8,128)(2,1)} %get-tuple-element.432), kind=kOutput, calls=%fused_computation.60 | convolution fusion | flops 11822694400 | bytes 99090432 | tf_op jit(solution)/shard_map/dot_general | solution.py:60
  792.2 1.9 fusion.62
  794.2 15.8 reduce-scatter.10.cloned.1.call-done
  810.0 2.9 fusion.69
  814.7 9.0 fusion.64
  825.5 9.6 fusion.66
  835.1 21.7 fusion.54
  857.3 5.5 collective-permute-done
  862.8 3.2 broadcast_select_fusion.5
  866.0 3.3 pad_maximum_fusion.2
  873.1 1092.6 %all-reduce.9.cloned.1.call-done = f32[2048,11264]{1,0:T(8,128)} async-done(((f32[2048,11264]{1,0:T(8,128)}), f32[2048,11264]{1,0:T(8,128)}) %all-reduce.9.cloned.1.call-update) | async-done | bytes 92274704
  1965.7 10.3 fusion.80
  1976.0 35.6 %reduce-scatter.14.cloned.1.call-done = f32[256,256]{1,0:T(8,128)} async-done(((f32[2048,256]{1,0:T(8,128)}), f32[256,256]{1,0:T(8,128)}) %reduce-scatter.14.cloned.1.call-update) | async-done | bytes 262160 | tf_op jit(solution)/shard_map/reduce_scatter | solution.py:285
  2011.6 44.4 %reduce-scatter.16.cloned.1.call-done = f32[256,256]{1,0:T(8,128)} async-done(((f32[2048,256]{1,0:T(8,128)}), f32[256,256]{1,0:T(8,128)}) %reduce-scatter.16.cloned.1.call-update) | async-done | bytes 262160 | tf_op jit(solution)/shard_map/reduce_scatter | solution.py:286
  2056.0 119.9 %reduce-scatter.12.cloned.1.call-done = f32[256,2048]{1,0:T(8,128)} async-done(((f32[2048,2048]{1,0:T(8,128)}), f32[256,2048]{1,0:T(8,128)}) %reduce-scatter.12.cloned.1.call-update) | async-done | bytes 2097168 | tf_op jit(solution)/shard_map/reduce_scatter | solution.py:284
  2175.9 119.8 %reduce-scatter.18.cloned.1.call-done = f32[256,2048]{1,0:T(8,128)} async-done(((f32[2048,2048]{1,0:T(8,128)}), f32[256,2048]{1,0:T(8,128)}) %reduce-scatter.18.cloned.1.call-update) | async-done | bytes 2097168 | tf_op jit(solution)/shard_map/reduce_scatter | solution.py:287
  2295.7 268.2 %reduce-scatter.20.cloned.1.call-done = f32[704,2048]{1,0:T(8,128)} async-done(((f32[5632,2048]{1,0:T(8,128)}), f32[704,2048]{1,0:T(8,128)}) %reduce-scatter.20.cloned.1.call-update) | async-done | bytes 5767184 | tf_op jit(solution)/shard_map/reduce_scatter | solution.py:198
  2564.0 4.9 broadcast_select_fusion.3
  2568.9 6.7 pad_maximum_fusion.1
  2578.8 248.5 %collective-permute-done.2 = bf16[4,704,2048]{2,1,0:T(8,128)(2,1)} collective-permute-done((bf16[4,704,2048]{2,1,0:T(8,128)(2,1)}, bf16[4,704,2048]{2,1,0:T(8,128)(2,1)}, u32[]{:S(2)}, u32[]{:S(2)}) %collective-permute-start.2) | collective-permute-done | bytes 11534368 | tf_op jit(solution)/shard_map/ppermute | solution.py:23
  2827.3 16.0 broadcast_select_fusion.1
  2843.4 19.9 pad_maximum_fusion
  2863.3 6.0 fusion.84
  2869.3 12.4 fusion.43
  2883.0 2.3 fusion.50
  2885.3 23.9 all-reduce.3
  2909.3 13.1 all-reduce.4
  2922.4 3.5 fusion.49
  2925.9 378.9 %all-reduce.11.cloned.1.call-done = (f32[256,2048]{1,0:T(8,128)}, f32[256,256]{1,0:T(8,128)}, f32[256,256]{1,0:T(8,128)}, f32[256,2048]{1,0:T(8,128)}, f32[256,5...) async-done(((f32[256,2048]{1,0:T(8,128)}, f32[256,256]{1,0:T(8,128)}, f32[256,256]{1,0:T(8,128)}, f32[256,2048]{1,0:T(8,128)}, f32[256,5632]{1,0:T(8,128)}, ...) | async-done | bytes 22020112 | tf_op jit(solution)/shard_map/psum | solution.py:291
  3304.8 3.3 copy.125
  3310.8 2.9 copy.129
  3315.5 2.8 copy.130
  3319.1 2.5 copy.131
  (626 shorter events, 288.4 us)
Async XLA Ops:
  7.2 28.9 all-gather.12.cloned.1.call-start
  7.9 53.6 %all-gather.14.cloned.1.call-start = ((), (), s32[]{:S(2)}) async-start(), calls=%async_computation.9 | async-start | bytes 1179648 | tf_op jit(solution)/shard_map/all_gather | solution.py:108
  8.7 109.2 %all-gather.10.cloned.1.call-start = ((), (), s32[]{:S(2)}) async-start(), calls=%async_computation.7 | async-start | bytes 9437184 | tf_op jit(solution)/shard_map/all_gather | solution.py:106
  9.4 217.0 %all-gather.16.cloned.1.call-start = ((), (), s32[]{:S(2)}) async-start(), calls=%async_computation.10 | async-start | bytes 9437184 | tf_op jit(solution)/shard_map/all_gather | solution.py:109
  10.0 282.3 %all-gather.18.cloned.1.call-start = ((), (), s32[]{:S(2)}) async-start(), calls=%async_computation.11 | async-start | bytes 25952256 | tf_op jit(solution)/shard_map/all_gather | solution.py:169
  10.6 1.6 copy-start.36
  10.6 12.0 copy-start
  10.6 399.9 %all-gather.20.cloned.1.call-start = ((), (), s32[]{:S(2)}) async-start(), calls=%async_computation.12 | async-start | bytes 25952256 | tf_op jit(solution)/shard_map/all_gather | solution.py:170
  11.2 11.7 copy-start.34
  11.2 11.7 copy-start.35
  11.2 11.9 copy-start.37
  11.2 517.7 %all-gather.22.cloned.1.call-start = ((), (), s32[]{:S(2)}) async-start(), calls=%async_computation.13 | async-start | bytes 25952256 | tf_op jit(solution)/shard_map/all_gather | solution.py:183
  11.9 778.5 %reduce-scatter.8.cloned.1.call-start = ((), (), s32[]{:S(2)}) async-start(), calls=%async_computation.14 | async-start | bytes 1310720 | tf_op jit(solution)/shard_map/reduce_scatter | solution.py:249
  22.6 107.7 %copy-start.27 = (f32[8,1,256]{2,1,0:T(1,128)}, f32[8,1,256]{2,1,0:T(1,128)S(1)}, u32[]{:S(2)}) copy-start(f32[8,1,256]{2,1,0:T(1,128)S(1)} %convert_element_type.151) | copy-start | bytes 24580
  22.9 107.4 %copy-start.31 = (f32[256]{0:T(256)}, f32[256]{0:T(256)S(1)}, u32[]{:S(2)}) copy-start(f32[256]{0:T(256)S(1)} %add_rsqrt_fusion.1) | copy-start | bytes 3076
  32.2 104.1 %copy-start.23 = (f32[256,32]{0,1:T(8,128)}, f32[256,32]{0,1:T(8,128)S(1)}, u32[]{:S(2)}) copy-start(f32[256,32]{0,1:T(8,128)S(1)} %get-tuple-element.446) | copy-start | bytes 98308
  32.2 104.1 %copy-start.25 = (f32[256,32]{0,1:T(8,128)}, f32[256,32]{0,1:T(8,128)S(1)}, u32[]{:S(2)}) copy-start(f32[256,32]{0,1:T(8,128)S(1)} %get-tuple-element.447) | copy-start | bytes 98308
  226.3 1.1 copy-start.10
  235.0 339.0 %copy-start.8 = (f32[256,2048]{1,0:T(8,128)}, f32[256,2048]{1,0:T(8,128)S(1)}, u32[]{:S(2)}) copy-start(f32[256,2048]{1,0:T(8,128)S(1)} %get-tuple-element.449) | copy-start | bytes 6291460
  235.2 175.3 %copy-start.14 = (bf16[256,2048]{1,0:T(8,128)(2,1)}, bf16[256,2048]{1,0:T(8,128)(2,1)S(1)}, u32[]{:S(2)}) copy-start(bf16[256,2048]{1,0:T(8,128)(2,1)S(1)} %multiply_convert_fusion.4) | copy-start | bytes 3145732
  559.9 14.0 copy-start.18
  576.1 1.3 copy-start.6
  754.4 55.5 %reduce-scatter.10.cloned.1.call-start = ((), (), s32[]{:S(2)}) async-start(), calls=%async_computation.15 | async-start | bytes 1310720 | tf_op jit(solution)/shard_map/reduce_scatter | solution.py:250
  755.2 1210.5 %all-reduce.9.cloned.1.call-start = ((), (), s32[]{:S(2)}) async-start(), calls=%async_computation.21 | async-start | bytes 184549376
  790.3 0.8 copy-start.24
  790.3 0.8 copy-start.26
  790.3 1.8 copy-start.1
  790.3 1.8 copy-start.28
  790.3 1.8 copy-start.32
  790.4 1221.2 %reduce-scatter.14.cloned.1.call-start = ((), (), s32[]{:S(2)}) async-start(), calls=%async_computation.17 | async-start | bytes 2359296 | tf_op jit(solution)/shard_map/reduce_scatter | solution.py:285
  794.1 19.2 copy-start.19
  794.1 1261.9 %reduce-scatter.16.cloned.1.call-start = ((), (), s32[]{:S(2)}) async-start(), calls=%async_computation.18 | async-start | bytes 2359296 | tf_op jit(solution)/shard_map/reduce_scatter | solution.py:286
  812.9 1363.1 %reduce-scatter.12.cloned.1.call-start = ((), (), s32[]{:S(2)}) async-start(), calls=%async_computation.16 | async-start | bytes 18874368 | tf_op jit(solution)/shard_map/reduce_scatter | solution.py:284
  813.7 1.0 copy-start.15
  823.8 1.7 copy-start.7
  823.8 1471.9 %reduce-scatter.18.cloned.1.call-start = ((), (), s32[]{:S(2)}) async-start(), calls=%async_computation.19 | async-start | bytes 18874368 | tf_op jit(solution)/shard_map/reduce_scatter | solution.py:287
  835.0 1728.9 %reduce-scatter.20.cloned.1.call-start = ((), (), s32[]{:S(2)}) async-start(), calls=%async_computation.20 | async-start | bytes 51904512 | tf_op jit(solution)/shard_map/reduce_scatter | solution.py:198
  856.8 2447.9 %all-reduce.11.cloned.1.call-start = ((), (), s32[]{:S(2)}) async-start(), calls=%async_computation.22 | async-start | bytes 44040192 | tf_op jit(solution)/shard_map/psum | solution.py:291
  857.1 5.7 collective-permute-start
  865.9 3.4 copy-start.4
  865.9 4.3 copy-start.5
  866.0 6.0 copy-start.38
  870.2 1693.8 %collective-permute-start.1 = (bf16[2,704,2048]{2,1,0:T(8,128)(2,1)}, bf16[2,704,2048]{2,1,0:T(8,128)(2,1)}, u32[]{:S(2)}, u32[]{:S(2)}) collective-permute-start(bf16[2,704,2048]{2,1,0:T(8,128)(2,1)} %pad_maximum_fusion.2), channel_id=1, source_target_pairs={{0,2},{1,3},{2,0},{3,1},{4,6},{5,7},{6,4},{7,5},{8,10},{9,11},{10,... | collective-permute-start | bytes 17301512 | tf_op jit(solution)/shard_map/ppermute | solution.py:23
  2568.9 6.8 copy-start.2
  2568.9 8.5 copy-start.3
  2577.4 249.9 %collective-permute-start.2 = (bf16[4,704,2048]{2,1,0:T(8,128)(2,1)}, bf16[4,704,2048]{2,1,0:T(8,128)(2,1)}, u32[]{:S(2)}, u32[]{:S(2)}) collective-permute-start(bf16[4,704,2048]{2,1,0:T(8,128)(2,1)} %pad_maximum_fusion.1), channel_id=1, source_target_pairs={{0,4},{1,5},{2,6},{3,7},{4,0},{5,1},{6,2},{7,3},{8,12},{9,13},{10,... | collective-permute-start | bytes 34603016 | tf_op jit(solution)/shard_map/ppermute | solution.py:23
  2843.4 19.9 copy-start.16
  2863.3 6.0 copy-start.9
  2863.3 6.0 copy-start.13
  2869.3 12.4 copy-start.17
  2881.7 1.0 copy-start.21
  2881.7 1.3 copy-start.22
  2883.0 2.3 copy-start.33
  3304.8 3.3 copy-start.30
  3304.8 4.0 copy-start.29
  3304.8 4.7 copy-start.20
  3304.8 6.0 copy-start.12
  3310.8 4.7 copy-start.11
  3310.8 7.5 slice-start
  3315.5 3.6 slice-start.1
Sparse Core Ops, SparseCore 0:
  9.9 26.1 all-gather.11
  38.0 23.4 all-gather.13
  63.4 54.3 all-gather.9
  119.6 54.3 all-gather.15
  175.7 116.4 all-gather.17
  294.0 116.4 all-gather.19
  412.4 116.4 all-gather.21
  754.6 27.1 reduce-scatter.7
  784.1 25.7 reduce-scatter.9
  813.6 1152.0 all-reduce.8
  1969.9 41.6 reduce-scatter.13
  2014.7 41.1 reduce-scatter.15
  2060.0 115.9 reduce-scatter.11
  2179.8 115.9 reduce-scatter.17
  2299.6 264.2 reduce-scatter.19
  2567.8 736.8 all-reduce.10
